TPU v7x, 256 devices: a whole 4x4x8 slice. The times are simulated.
256 devices in a mesh: pair: 16 (over z, core), red: 16 (over x, y).
Axes of the slice: x: 4, y: 4, z: 8, core: 2. Of those that a mesh axis runs over, the one named last changes fastest.
Arguments:
- three_center: bfloat16 [2304, 256, 256], P('pair', 'red'), may hold values from -0.375 to 0.375
- occ_src: int32 [256, 16], P('red'), may hold values from 0 to 15, as said below
- occ_block: int32 [256, 16], P('red'), may hold values from 0 to 31
- occ_blocks: bfloat16 [512, 256], P('red'), may hold values from -0.375 to 0.375
- virt_block: int32 [16, 16, 1], P('red'), may hold values from 0 to 31, as said below
- virt_blocks: bfloat16 [16, 32, 256], P('red', 'pair'), may hold values from -1.5 to 1.5
Outputs:
- chi: float32 [2304, 2304], P('pair', 'red')
Inputs may be any that keep to these rules, and one draw needn't show every extreme that they name: `occ_src`: the 16 entries of a row are distinct. `virt_block`: every block listed for tile t of a red group lies from (t) * 2 to (t) * 2 + 1.
All inputs are finite; a program needn't handle non-finite values.
Results may differ from a plain program's by a relative error of at most 0.0041.
Values may be sent and summed in bfloat16 or wider, within the bound.
A program may use at most 128 MiB of HBM per device.

v0:
```python
import jax
import jax.numpy as jnp
from jax import lax
from jax.sharding import PartitionSpec as P

BLK = 16
TPD = 1


def occupied(three_center, occ_src, occ_block, occ_blocks):
    aux_rows, ntiles, area = three_center.shape
    nblocks = occ_blocks.shape[0]
    block_hot = (
        occ_block[:, :, None] == jnp.arange(nblocks, dtype=jnp.int32)[None, None, :]
    ).astype(jnp.bfloat16)
    picked = jnp.einsum(
        "tsb,bk->tsk", block_hot, occ_blocks, preferred_element_type=jnp.float32
    ).astype(jnp.bfloat16)
    source_hot = (occ_src[:, :, None] == jnp.arange(ntiles, dtype=jnp.int32)[None, None, :]).astype(
        jnp.bfloat16
    )
    mixing = jnp.einsum(
        "tsk,tsa->tka", source_hot, picked, preferred_element_type=jnp.float32
    ).astype(jnp.bfloat16)
    mixing = mixing.reshape(ntiles, ntiles, BLK, BLK)
    blocks = three_center.reshape(aux_rows, ntiles, BLK, BLK)
    half = jnp.einsum("tkml,pkln->ptmn", mixing, blocks, preferred_element_type=jnp.float32)
    return half.reshape(aux_rows, ntiles, area).astype(jnp.bfloat16)


def virtual(half, listed, blocks):
    aux_rows, ntiles, area = half.shape
    owners = listed.shape[0]
    nblocks = blocks.shape[0]
    block_hot = (listed[..., None] == jnp.arange(nblocks, dtype=jnp.int32)).astype(jnp.bfloat16)
    picked = jnp.einsum(
        "oijb,bk->oijk", block_hot, blocks, preferred_element_type=jnp.float32
    ).astype(jnp.bfloat16)
    picked = picked.reshape(owners, TPD, TPD, BLK, BLK)
    grouped = half.reshape(aux_rows, owners, TPD, BLK, BLK)
    kernel = jnp.einsum("pojml,oijln->poimn", grouped, picked, preferred_element_type=jnp.float32)
    return kernel.reshape(aux_rows, ntiles, area).astype(jnp.bfloat16)


def shards(three_center, occ_src, occ_block, occ_blocks, virt_block, virt_blocks):
    aux_rows, ntiles, area = three_center.shape
    half = occupied(three_center, occ_src, occ_block, occ_blocks)
    own_blocks = virt_blocks[0]
    listed = virt_block[0]
    all_blocks = lax.all_gather(own_blocks, "pair", axis=0, tiled=True)
    kernel = virtual(half, listed.reshape(ntiles // TPD, TPD, TPD), all_blocks)
    flat_tiles = three_center.reshape(aux_rows, ntiles * area)
    piece = lax.all_gather(kernel, "pair", axis=0, tiled=True)
    flat_piece = piece.reshape(piece.shape[0], ntiles * area)
    partial_value = lax.dot_general(
        flat_tiles, flat_piece, (((1,), (1,)), ((), ())), preferred_element_type=jnp.float32
    )
    return lax.psum_scatter(partial_value, "red", scatter_dimension=1, tiled=True)


def solution(mesh):
    placed = (
        P("pair", "red", None),
        P("red", None),
        P("red", None),
        P("red", None),
        P("red", None, None),
        P("red", "pair", None),
    )
    return jax.shard_map(
        shards, mesh=mesh, in_specs=placed, out_specs=P("pair", "red"), check_vma=False
    )
```

profile of v0, /device:TPU:4, one launch (start us, length us, event | category | flops | bytes accessed | tf_op | source)
XLA Modules:
  0.0 243.2 jit_solution(1345893647742258906)
XLA Ops:
  6.5 0.0 copy-start
  6.5 0.0 copy-start.1
  6.5 0.0 all-gather.3.cloned.1.call-start
  6.5 0.8 copy.21
  7.3 20.0 %all-gather = bf16[1,32,256]{2,0,1:T(2,128)(2,1)S(1)} all-gather(bf16[1,2,256]{2,0,1:T(2,128)(2,1)S(1)} %copy.21), channel_id=2, replica_groups=mesh['pair'=16,'red'=16] {'pair'}, dimensions={1}, use_global_device_ids=true | all-gather | bytes 17408 | tf_op jit(solution)/shard_map/all_gather | solution.py:50
  27.4 0.8 convolution_convert_fusion.2
  28.2 0.1 reshape.42
  28.3 0.0 copy-done
  28.3 1.1 convolution_convert_fusion
  29.4 1.7 reshape.47
  31.1 0.0 copy-done.1
  31.1 1.2 copy.22
  32.3 3.4 %fusion.7 = bf16[144,16,16,16]{0,2,3,1:T(8,128)(2,1)S(1)} fusion(bf16[144,16,16,16]{0,3,2,1:T(8,128)(2,1)S(1)} %bitcast.43, bf16[16,16,16,16,1]{3,2,1,0,4:T(8,128)(2,1)} %reshape.47), kind=kOutput, calls=%fused_computation.7 | convolution fusion | flops 302579712 | bytes 2490368 | tf_op jit(solution)/shard_map/tkml,pkln->ptmn/dot_general | solution.py:27
  35.7 2.2 fusion.4
  37.9 3.7 %copy.26 = bf16[144,16,256]{2,0,1:T(8,128)(2,1)} copy(bf16[144,16,256]{0,2,1:T(8,128)(2,1)} %bitcast.44) | data formatting | bytes 2359296 | tf_op jit(solution)/shard_map/convert_element_type | solution.py:42
  41.5 0.0 all-gather.3.cloned.1.call-update
  41.6 0.0 reduce-scatter.4.cloned.1.call-start
  41.6 103.5 %all-gather.3.cloned.1.call-done = bf16[2304,16,256]{2,0,1:T(8,128)(2,1)} async-done(((bf16[144,16,256]{2,0,1:T(8,128)(2,1)}), bf16[2304,16,256]{2,0,1:T(8,128)(2,1)}) %all-gather.3.cloned.1.call-update) | async-done | bytes 18874384 | tf_op jit(solution)/shard_map/all_gather | solution.py:53
  145.1 9.5 %convolution_bitcast_fusion = f32[144,2304]{1,0:T(8,128)S(1)} fusion(bf16[2304,16,256]{2,0,1:T(8,128)(2,1)} %all-gather.3.cloned.1.call-done, bf16[144,16,256]{0,2,1:T(8,128)(2,1)S(1)} %copy.22), kind=kOutput, calls=%fused_computation.1 | convolution fusion | flops 2717908992 | bytes 21381120 | tf_op jit(solution)/shard_map/dot_general | solution.py:55
  154.6 1.9 copy.33
  156.5 0.0 reduce-scatter.4.cloned.1.call-update
  156.5 78.2 %reduce-scatter.4.cloned.1.call-done = f32[144,144]{1,0:T(8,128)} async-done(((f32[2304,144]{1,0:T(8,128)}), f32[144,144]{1,0:T(8,128)}) %reduce-scatter.4.cloned.1.call-update) | async-done | bytes 82960
  234.7 1.7 copy.34
Async XLA Ops:
  6.5 21.8 %copy-start = (bf16[32,256]{1,0:T(8,128)(2,1)S(1)}, bf16[32,256]{1,0:T(8,128)(2,1)}, u32[]{:S(2)}) copy-start(bf16[32,256]{1,0:T(8,128)(2,1)} %param.9) | copy-start | bytes 49156
  6.5 24.5 %copy-start.1 = (bf16[144,16,256]{2,1,0:T(8,128)(2,1)S(1)}, bf16[144,16,256]{2,1,0:T(8,128)(2,1)}, u32[]{:S(2)}) copy-start(bf16[144,16,256]{2,1,0:T(8,128)(2,1)} %param.6) | copy-start | bytes 3538948
  6.5 138.5 %all-gather.3.cloned.1.call-start = ((), (), s32[]{:S(2)}) async-start(), calls=%async_computation.1 | async-start | bytes 20054016 | tf_op jit(solution)/shard_map/all_gather | solution.py:53
  41.6 193.2 %reduce-scatter.4.cloned.1.call-start = ((), (), s32[]{:S(2)}) async-start(), calls=%async_computation.2 | async-start | bytes 2506752
Sparse Core Ops, SparseCore 0:
  41.7 103.3 all-gather.2
  156.6 78.0 reduce-scatter.3
where the time goes:
time: 244 us; the launch traced here: 243 us
  waiting for transfers between devices  182 us (75%)
  blocking collectives  20 us (8%)
  matrix products  17 us (7%)
  between operations  13.4 us (5%)
  local copies, waits for them, and re-layouts  11 us (5%)
    all_gather x1, waiting for transfers between devices, shards(): piece = lax.all_gather(kernel, 'pair', axis=0, tiled=True)  103 us
    unnamed x3, waiting for transfers between devices  78.3 us
    all_gather x1, blocking collectives, shards(): all_blocks = lax.all_gather(own_blocks, 'pair', axis=0, tiled=True)  20 us
    dot_general x1, matrix products, shards(): lax.dot_general(flat_tiles, flat_piece, (((1,), (1,)), ((), ())), preferr...  9.48 us
    unnamed x8, local copies, waits for them, and re-layouts  5.55 us
  transfers between devices with their start and end apart: 2, of which 2 were waited for; matrix products, arithmetic and copies ran while one was open for 0% of the time, Pallas kernels for 0%

commit v1 on v0

v1 whole, which is shorter than its diff:
```python
import jax
import jax.numpy as jnp
from jax import lax
from jax.experimental import pallas as pl
from jax.experimental.pallas import tpu as pltpu
from jax.sharding import PartitionSpec as P

BLK = 16
MESH = pl.DeviceIdType.MESH
CHUNKS = 3
OFFSETS = (0, -1, 2, 3, 0, 1, -2, -3)
PAIRS = (
    (0, 0), (4, 0),
    (2, 0), (6, 0), (0, 2), (6, 2),
    (3, 0), (7, 0), (3, 2), (7, 2),
    (1, 0), (5, 0), (1, 2), (5, 2),
    (1, 3), (7, 3),
)


def mixing_matrix(occ_src, occ_block, occ_blocks):
    ntiles = occ_src.shape[0]
    nblocks = occ_blocks.shape[0]
    block_hot = (
        occ_block[:, :, None] == jnp.arange(nblocks, dtype=jnp.int32)[None, None, :]
    ).astype(jnp.bfloat16)
    picked = jnp.einsum(
        "tsb,bk->tsk", block_hot, occ_blocks, preferred_element_type=jnp.float32
    ).astype(jnp.bfloat16)
    source_hot = (occ_src[:, :, None] == jnp.arange(ntiles, dtype=jnp.int32)[None, None, :]).astype(
        jnp.bfloat16
    )
    mixing = jnp.einsum(
        "tsk,tsa->tka", source_hot, picked, preferred_element_type=jnp.float32
    ).astype(jnp.bfloat16)
    mixing = mixing.reshape(ntiles, ntiles, BLK, BLK)
    return mixing.transpose(1, 3, 0, 2).reshape(ntiles * BLK, ntiles * BLK)


def kernel(
    tiles_hbm, mix_ref, virt_ref, out_ref,
    rows, wide, xs, kv, virt, kern, sendbuf, recvbuf,
    far_send, far_recv, fwd_send, fwd_recv, near_send, near_recv,
    sib_send, sib_recv, virt_send, virt_recv, part_send, part_recv, local_sem,
):
    naux = tiles_hbm.shape[0]
    ntiles = 16
    area = 256
    step_rows = naux // CHUNKS
    me = lax.axis_index("pair")
    red = lax.axis_index("red")
    z, core = me // 2, me % 2
    sign = 1 - 2 * core

    def at(offset, which):
        return ((z + sign * offset + 16) % 8) * 2 + which

    col_z, col_core = red // 2, red % 2
    csign = 1 - 2 * col_core
    delta = (csign * (z - col_z) + 16) % 8
    same = core == col_core
    col_off_same = jnp.where(delta == 4, 3, jnp.where((delta == 5) | (delta == 6) | (delta == 1), 2, 0))
    col_off_other = jnp.where(delta == 2, 3, jnp.where((delta == 3) | (delta == 4) | (delta == 7), 2, 0))
    col_off = jnp.where(same, col_off_same, col_off_other)
    maker = ((col_z - csign * col_off + 16) % 8) * 2 + col_core

    barrier = pltpu.get_barrier_semaphore()

    def greet(o, c):
        pl.semaphore_signal(barrier, inc=1, device_id=((me + o) % 16, red), device_id_type=MESH)
        return c

    lax.fori_loop(1, 16, greet, 0)

    def greet_maker(g, c):
        own = (maker == me) & (g == red)

        @pl.when(jnp.logical_not(own))
        def _():
            pl.semaphore_signal(barrier, inc=1, device_id=(maker, g), device_id_type=MESH)

        return c

    lax.fori_loop(0, 16, greet_maker, 0)
    pl.semaphore_wait(barrier, 31 - jnp.where(maker == me, 1, 0))

    def slot(i):
        return rows.at[pl.ds(i * naux, naux), :]

    def piece(i, c):
        return rows.at[pl.ds(i * naux + c * step_rows, step_rows), :]

    far = []
    for c in range(CHUNKS):
        copy = pltpu.make_async_remote_copy(
            src_ref=tiles_hbm.at[pl.ds(c * step_rows, step_rows), :], dst_ref=piece(2, c),
            send_sem=far_send.at[c], recv_sem=far_recv.at[c],
            device_id=(at(-2, core), red), device_id_type=MESH,
        )
        copy.start()
        far.append(copy)
    own_copy = pltpu.make_async_copy(tiles_hbm, slot(0), local_sem.at[0])
    own_copy.start()
    own_virt = pltpu.make_async_copy(virt_ref, virt.at[me], local_sem.at[1])
    own_virt.start()

    def virt_copy(o):
        return pltpu.make_async_remote_copy(
            src_ref=virt_ref, dst_ref=virt.at[me],
            send_sem=virt_send.at[o], recv_sem=virt_recv.at[me],
            device_id=((me + o) % 16, red), device_id_type=MESH,
        )

    def virt_start(o, c):
        virt_copy(o).start()
        return c

    lax.fori_loop(1, 16, virt_start, 0)

    def sibling(i, src):
        return pltpu.make_async_remote_copy(
            src_ref=src, dst_ref=slot(4 + i),
            send_sem=sib_send.at[i], recv_sem=sib_recv.at[i],
            device_id=(z * 2 + 1 - core, red), device_id_type=MESH,
        )

    sib = [sibling(0, tiles_hbm)] + [sibling(i, slot(i)) for i in (1, 2, 3)]
    sib[0].start()
    near = pltpu.make_async_remote_copy(
        src_ref=tiles_hbm, dst_ref=slot(1), send_sem=near_send.at[0], recv_sem=near_recv.at[0],
        device_id=(at(1, core), red), device_id_type=MESH,
    )
    fwd = [
        pltpu.make_async_remote_copy(
            src_ref=piece(2, c), dst_ref=piece(3, c),
            send_sem=fwd_send.at[c], recv_sem=fwd_recv.at[c],
            device_id=(at(-1, core), red), device_id_type=MESH,
        )
        for c in range(CHUNKS)
    ]

    lane = lax.broadcasted_iota(jnp.int32, (BLK, area), 1)
    sub = lax.broadcasted_iota(jnp.int32, (BLK, area), 0)
    keep = (lane % BLK) == sub
    grow = lax.broadcasted_iota(jnp.int32, (area, area), 0)
    glane = lax.broadcasted_iota(jnp.int32, (area, area), 1)

    def widen(t, c):
        pick = (grow == t * BLK + glane // BLK).astype(jnp.float32).astype(jnp.bfloat16)
        xs[...] = jnp.dot(mix_ref[...], pick, preferred_element_type=jnp.float32)

        def group(q, c2):
            base = q * 16
            for r in range(16):
                row = xs[pl.ds(base + r, 1), :]
                value = jnp.where(keep, jnp.broadcast_to(row, (BLK, area)), 0.0)
                wide[t, pl.ds(pl.multiple_of((base + r) * BLK, BLK), BLK), :] = value.astype(jnp.bfloat16)
            return c2

        lax.fori_loop(0, area // 16, group, 0)
        return c

    lax.fori_loop(0, ntiles, widen, 0)

    own_virt.wait()

    def virt_wait(o, c):
        src = (me + o) % 16
        pltpu.make_async_remote_copy(
            src_ref=virt_ref, dst_ref=virt.at[src],
            send_sem=virt_send.at[o], recv_sem=virt_recv.at[src],
            device_id=(src, red), device_id_type=MESH,
        ).wait()
        return c

    lax.fori_loop(1, 16, virt_wait, 0)
    diagonal = (grow // BLK) == (glane // BLK)

    def spread(t, c):
        block = virt[t].astype(jnp.float32)
        tall = jnp.concatenate([block] * BLK, axis=0)
        kv[t] = jnp.where(diagonal, tall, 0.0).astype(jnp.bfloat16)
        return c

    lax.fori_loop(0, ntiles, spread, 0)

    def make_kernel(first, count, begin, end):
        def tile(t, c):
            half = jnp.dot(
                rows[first * naux:(first + count) * naux, :], wide[t], preferred_element_type=jnp.float32
            ).astype(jnp.bfloat16)
            value = jnp.dot(half, kv[t], preferred_element_type=jnp.float32).astype(jnp.bfloat16)
            k0 = {0: 0, 2: 1, 3: 2}[first]
            kern[k0 * naux:(k0 + count) * naux, pl.ds(pl.multiple_of(t * area, area), area)] = value
            return c

        lax.fori_loop(begin, end, tile, 0)

    def product(n):
        row_slot, col_slot = PAIRS[n]
        k0 = {0: 0, 2: 1, 3: 2}[col_slot]
        value = lax.dot_general(
            rows[row_slot * naux:(row_slot + 1) * naux, :], kern[k0 * naux:(k0 + 1) * naux, :],
            (((1,), (1,)), ((), ())), preferred_element_type=jnp.float32,
        )
        sendbuf[n] = value.astype(jnp.bfloat16)
        to_pair = at(OFFSETS[row_slot], core if row_slot < 4 else 1 - core)
        to_red = at(OFFSETS[col_slot], core)
        own = (to_pair == me) & (to_red == red)

        @pl.when(own)
        def _():
            pltpu.make_async_copy(sendbuf.at[n], recvbuf.at[red], part_recv.at[red]).start()

        @pl.when(jnp.logical_not(own))
        def _():
            pltpu.make_async_remote_copy(
                src_ref=sendbuf.at[n], dst_ref=recvbuf.at[red],
                send_sem=part_send.at[n], recv_sem=part_recv.at[red],
                device_id=(to_pair, to_red), device_id_type=MESH,
            ).start()

    own_copy.wait()

    def relay(c):
        far[c].wait_recv()
        fwd[c].start()

    relay(0)
    make_kernel(0, 1, 0, 8)
    relay(1)
    near.start()
    make_kernel(0, 1, 8, 16)
    relay(2)
    sib[2].start()
    sib[0].wait_recv()
    product(0)
    product(1)
    make_kernel(2, 1, 0, 16)
    sib[2].wait_recv()
    for n in range(2, 6):
        product(n)
    for c in range(CHUNKS):
        fwd[c].wait_recv()
    sib[3].start()
    near.wait_recv()
    sib[1].start()
    make_kernel(3, 1, 0, 16)
    sib[3].wait_recv()
    sib[1].wait_recv()
    for n in range(6, 16):
        product(n)

    total = jnp.zeros((naux, naux), jnp.float32)
    for g in range(16):
        pltpu.make_async_copy(sendbuf.at[0], recvbuf.at[g], part_recv.at[g]).wait()
    for g in range(16):
        total = total + recvbuf[g].astype(jnp.float32)
    out_ref[...] = total

    for c in range(CHUNKS):
        far[c].wait_send()
        fwd[c].wait_send()
    near.wait_send()
    for copy in sib:
        copy.wait_send()
    for n in range(16):
        row_slot, col_slot = PAIRS[n]
        to_pair = at(OFFSETS[row_slot], core if row_slot < 4 else 1 - core)
        to_red = at(OFFSETS[col_slot], core)
        own = (to_pair == me) & (to_red == red)

        @pl.when(jnp.logical_not(own))
        def _(n=n, to_pair=to_pair, to_red=to_red):
            pltpu.make_async_remote_copy(
                src_ref=sendbuf.at[n], dst_ref=recvbuf.at[red],
                send_sem=part_send.at[n], recv_sem=part_recv.at[red],
                device_id=(to_pair, to_red), device_id_type=MESH,
            ).wait_send()


def shards(three_center, occ_src, occ_block, occ_blocks, virt_block, virt_blocks):
    naux, ntiles, area = three_center.shape
    tiles = three_center.reshape(naux, ntiles * area)
    mix = mixing_matrix(occ_src, occ_block, occ_blocks)
    me = lax.axis_index("pair")
    listed = lax.dynamic_index_in_dim(virt_block[0, :, 0], me, keepdims=False) - 2 * me
    held = virt_blocks[0]
    block = jnp.where(listed == 0, held[0], held[1]).reshape(BLK, BLK)
    virt = jnp.tile(block, (1, BLK))
    dma = pltpu.SemaphoreType.DMA
    bf16 = jnp.bfloat16
    return pl.pallas_call(
        kernel,
        out_shape=jax.ShapeDtypeStruct((naux, naux), jnp.float32),
        in_specs=[
            pl.BlockSpec(memory_space=pl.ANY),
            pl.BlockSpec(memory_space=pltpu.VMEM),
            pl.BlockSpec(memory_space=pltpu.VMEM),
        ],
        out_specs=pl.BlockSpec(memory_space=pltpu.VMEM),
        scratch_shapes=[
            pltpu.VMEM((8 * naux, ntiles * area), bf16),
            pltpu.VMEM((ntiles, ntiles * area, area), bf16),
            pltpu.VMEM((area, area), jnp.float32),
            pltpu.VMEM((ntiles, area, area), bf16),
            pltpu.VMEM((ntiles, BLK, area), bf16),
            pltpu.VMEM((3 * naux, ntiles * area), bf16),
            pltpu.VMEM((16, naux, naux), bf16),
            pltpu.VMEM((16, naux, naux), bf16),
            dma((CHUNKS,)), dma((CHUNKS,)), dma((CHUNKS,)), dma((CHUNKS,)), dma((1,)), dma((1,)),
            dma((4,)), dma((4,)), dma((16,)), dma((16,)), dma((16,)), dma((16,)), dma((2,)),
        ],
        compiler_params=pltpu.CompilerParams(
            collective_id=0, has_side_effects=True, vmem_limit_bytes=64000000
        ),
    )(tiles, mix, virt)


def solution(mesh):
    placed = (
        P("pair", "red", None),
        P("red", None),
        P("red", None),
        P("red", None),
        P("red", None, None),
        P("red", "pair", None),
    )
    return jax.shard_map(
        shards, mesh=mesh, in_specs=placed, out_specs=P("pair", "red"), check_vma=False
    )
```

time: 244 us -> 123 us (0.50)
  the two profiles are of different devices: /device:TPU:4 before, /device:TPU:7 now
where the time goes in v1:
time: 123 us
  Pallas kernels  112 us (91%)
  local copies, waits for them, and re-layouts  8.51 us (7%)
    pallas_call x1, Pallas kernels, shards(): pl.pallas_call(kernel, out_shape=jax.ShapeDtypeStruct((naux, naux), jnp.f...  112 us
    unnamed x6, local copies, waits for them, and re-layouts  3.08 us

profile of v1, /device:TPU:7, one launch (start us, length us, event | category | flops | bytes accessed | tf_op | source)
XLA Modules:
  0.0 122.8 jit_solution(14109530133767244671)
XLA Ops:
  0.0 0.0 copy-start
  0.0 1.2 %constant_dynamic-slice_fusion = s32[1,1,1]{1,2,0:T(1,128)} fusion(s32[1,16,1]{1,2,0:T(1,128)} %param.10, s32[]{:T(128)S(6)} %select_n.19), kind=kLoop, calls=%fused_computation.9 | loop fusion | bytes 12 | tf_op jit(solution)/shard_map/jit(dynamic_index_in_dim)/dynamic_slice | solution.py:287
  1.9 0.8 fusion.5
  2.7 0.1 select_n.22
  2.8 0.7 tile.9.virt_ref
  3.5 0.0 copy-done
  3.5 1.1 convolution_convert_fusion
  4.6 0.7 reshape.32
  5.3 0.0 copy-start.1
  5.3 1.0 copy.7
  6.3 1.7 %reshape.33.mix_ref = bf16[256,256]{1,0:T(8,128)(2,1)} reshape(bf16[16,16,16,16]{3,2,1,0:T(8,128)(2,1)S(1)} %bitcast.11) | data formatting | bytes 262144 | tf_op jit(solution)/shard_map/reshape | solution.py:37
  8.0 0.0 copy-done.1
  8.0 1.5 %copy.8 = bf16[18,8,16,256]{3,1,2,0:T(8,128)(2,1)} copy(bf16[18,8,16,256]{3,2,1,0:T(8,128)(2,1)S(1)} %bitcast.12) | data formatting | bytes 2359296
  9.5 111.7 %shard_map.64 = f32[144,144]{1,0:T(8,128)} custom-call(bf16[144,4096]{1,0:T(8,128)(2,1)} %bitcast.10, bf16[256,256]{1,0:T(8,128)(2,1)} %reshape.33.mix_ref, bf16[16,256]{1,0:T(8,128)(2,1)} %tile.9.virt_ref), custom_call_target="tpu_custom_call" | custom-call | tf_op jit(solution)/shard_map/pallas_call | solution.py:293
  121.2 1.6 %copy.10 = f32[144,144]{1,0:T(8,128)} copy(f32[144,144]{1,0:T(8,128)} %shard_map.64) | data formatting | bytes 165888
  (1 shorter events, 0.0 us)
Async XLA Ops:
  0.0 3.5 %copy-start = (bf16[32,256]{1,0:T(8,128)(2,1)S(1)}, bf16[32,256]{1,0:T(8,128)(2,1)}, u32[]{:S(2)}) copy-start(bf16[32,256]{1,0:T(8,128)(2,1)} %param.9) | copy-start | bytes 49156
  5.3 2.7 %copy-start.1 = (bf16[144,16,256]{2,1,0:T(8,128)(2,1)S(1)}, bf16[144,16,256]{2,1,0:T(8,128)(2,1)}, u32[]{:S(2)}) copy-start(bf16[144,16,256]{2,1,0:T(8,128)(2,1)} %param.6) | copy-start | bytes 3538948

commit v2 on v1

v2 whole, which is shorter than its diff:
```python
import jax
import jax.numpy as jnp
from jax import lax
from jax.experimental import pallas as pl
from jax.experimental.pallas import tpu as pltpu
from jax.sharding import PartitionSpec as P

BLK = 16
MESH = pl.DeviceIdType.MESH
CHUNKS = 3
OFFSETS = (0, -1, 2, 3, 0, 1, -2, -3)
PAIRS = (
    (0, 0), (4, 0),
    (2, 0), (6, 0), (0, 2), (6, 2),
    (3, 0), (7, 0), (3, 2), (7, 2), (7, 3),
    (1, 0), (5, 0), (1, 2), (5, 2), (1, 3),
)


def kernel(
    tiles_hbm, src_ref, block_ref, occ_ref, listed_ref, virt_ref, out_ref,
    rows, wide, xs, mix, kv, virt, kern, sendbuf, recvbuf, summed, arrived,
    far_send, far_recv, fwd_send, fwd_recv, near_send, near_recv, near_sib_send, near_sib_recv,
    sib_send, sib_recv, virt_send, virt_recv, part_send, part_recv, local_sem, final_sem,
):
    naux = tiles_hbm.shape[0]
    ntiles = 16
    area = 256
    step_rows = naux // CHUNKS
    me = lax.axis_index("pair")
    red = lax.axis_index("red")
    z, core = me // 2, me % 2
    sign = 1 - 2 * core

    def at(offset, which):
        return ((z + sign * offset + 16) % 8) * 2 + which

    row_off, row_core, col_off = 0, core, 0
    for n, (row_slot, col_slot) in enumerate(PAIRS):
        here = red == n
        row_off = jnp.where(here, OFFSETS[row_slot], row_off)
        row_core = jnp.where(here, core if row_slot < 4 else 1 - core, row_core)
        col_off = jnp.where(here, OFFSETS[col_slot], col_off)
    to_pair, to_red = at(row_off, row_core), at(col_off, core)

    col_z, col_core = red // 2, red % 2
    col_sign = 1 - 2 * col_core
    delta = (col_sign * (z - col_z) + 16) % 8
    other = (core + col_core) % 2
    maker, adder = me, red
    for n, (row_slot, col_slot) in enumerate(PAIRS):
        here = (delta == (OFFSETS[row_slot] - OFFSETS[col_slot]) % 8) & (other == row_slot // 4)
        maker = jnp.where(here, ((col_z - col_sign * OFFSETS[col_slot] + 16) % 8) * 2 + col_core, maker)
        adder = jnp.where(here, n, adder)

    barrier = pltpu.get_barrier_semaphore()

    def greet(o, c):
        pl.semaphore_signal(barrier, inc=1, device_id=((me + o) % 16, red), device_id_type=MESH)
        return c

    lax.fori_loop(1, 16, greet, 0)

    def greet_plane(o, c):
        pl.semaphore_signal(barrier, inc=1, device_id=(me, (red + o) % 16), device_id_type=MESH)
        return c

    lax.fori_loop(1, 16, greet_plane, 0)
    stays = (maker == me) & (adder == red)

    @pl.when(jnp.logical_not(stays))
    def _():
        pl.semaphore_signal(barrier, inc=1, device_id=(maker, adder), device_id_type=MESH)

    pl.semaphore_wait(barrier, 31 - jnp.where(stays, 1, 0))

    def slot(i):
        return rows.at[pl.ds(i * naux, naux), :]

    def piece(i, c):
        return rows.at[pl.ds(i * naux + c * step_rows, step_rows), :]

    far = []
    for c in range(CHUNKS):
        copy = pltpu.make_async_remote_copy(
            src_ref=tiles_hbm.at[pl.ds(c * step_rows, step_rows), :], dst_ref=piece(2, c),
            send_sem=far_send.at[c], recv_sem=far_recv.at[c],
            device_id=(at(-2, core), red), device_id_type=MESH,
        )
        copy.start()
        far.append(copy)
    own_copy = pltpu.make_async_copy(tiles_hbm, slot(0), local_sem.at[0])
    own_copy.start()
    own_virt = pltpu.make_async_copy(virt_ref.at[0], virt.at[me], local_sem.at[1])
    own_virt.start()

    def virt_copy(o):
        return pltpu.make_async_remote_copy(
            src_ref=virt_ref.at[0], dst_ref=virt.at[me],
            send_sem=virt_send.at[o], recv_sem=virt_recv.at[me],
            device_id=((me + o) % 16, red), device_id_type=MESH,
        )

    def virt_start(o, c):
        virt_copy(o).start()
        return c

    lax.fori_loop(1, 16, virt_start, 0)

    def sibling(i, src):
        return pltpu.make_async_remote_copy(
            src_ref=src, dst_ref=slot(4 + i),
            send_sem=sib_send.at[i], recv_sem=sib_recv.at[i],
            device_id=(z * 2 + 1 - core, red), device_id_type=MESH,
        )

    sib = {0: sibling(0, tiles_hbm), 2: sibling(2, slot(2)), 3: sibling(3, slot(3))}
    sib[0].start()
    near, near_sib = [], []
    for c in range(CHUNKS):
        near.append(pltpu.make_async_remote_copy(
            src_ref=tiles_hbm.at[pl.ds(c * step_rows, step_rows), :], dst_ref=piece(1, c),
            send_sem=near_send.at[c], recv_sem=near_recv.at[c],
            device_id=(at(1, core), red), device_id_type=MESH,
        ))
        near_sib.append(pltpu.make_async_remote_copy(
            src_ref=piece(1, c), dst_ref=piece(5, c),
            send_sem=near_sib_send.at[c], recv_sem=near_sib_recv.at[c],
            device_id=(z * 2 + 1 - core, red), device_id_type=MESH,
        ))
    fwd = [
        pltpu.make_async_remote_copy(
            src_ref=piece(2, c), dst_ref=piece(3, c),
            send_sem=fwd_send.at[c], recv_sem=fwd_recv.at[c],
            device_id=(at(-1, core), red), device_id_type=MESH,
        )
        for c in range(CHUNKS)
    ]

    lane = lax.broadcasted_iota(jnp.int32, (BLK, area), 1)
    sub = lax.broadcasted_iota(jnp.int32, (BLK, area), 0)
    keep = (lane % BLK) == sub
    grow = lax.broadcasted_iota(jnp.int32, (area, area), 0)
    glane = lax.broadcasted_iota(jnp.int32, (area, area), 1)

    same_group = (grow // BLK) == (glane // BLK)
    same_place = (grow % BLK) == (glane % BLK)
    across = same_group.astype(jnp.float32).astype(jnp.bfloat16)
    along = same_place.astype(jnp.float32).astype(jnp.bfloat16)
    trow = lax.broadcasted_iota(jnp.int32, (area, BLK), 0)
    tlane = lax.broadcasted_iota(jnp.int32, (area, BLK), 1)
    repeat = (trow // BLK == tlane).astype(jnp.float32).astype(jnp.bfloat16)
    place = (trow % BLK) == tlane

    def taller(x):
        return jnp.dot(repeat, x, preferred_element_type=jnp.float32)

    fed = taller(src_ref[...].astype(jnp.float32).astype(jnp.bfloat16))
    fed_hot = (fed == (trow % BLK).astype(jnp.float32)).astype(jnp.float32).astype(jnp.bfloat16)
    lanes_of = (lane % BLK == sub).astype(jnp.float32).astype(jnp.bfloat16)
    fed_wide = jnp.where(same_group, jnp.dot(fed_hot, lanes_of, preferred_element_type=jnp.float32), 0.0)
    used = taller(block_ref[...].astype(jnp.float32).astype(jnp.bfloat16))
    used = jnp.sum(jnp.where(place, used, 0.0), axis=1, keepdims=True)
    nblocks = occ_ref.shape[0]
    number = lax.broadcasted_iota(jnp.int32, (area, nblocks), 1).astype(jnp.float32)
    used_hot = (used == number).astype(jnp.float32).astype(jnp.bfloat16)
    picked = jnp.dot(used_hot, occ_ref[...], preferred_element_type=jnp.float32).astype(jnp.bfloat16)
    mix[...] = jnp.dot(
        fed_wide.astype(jnp.bfloat16), picked, preferred_element_type=jnp.float32
    ).astype(jnp.bfloat16)

    def widen(t, c):
        tall = taller(mix[pl.ds(pl.multiple_of(t * BLK, BLK), BLK), :])
        tall = jnp.where(same_place, tall, 0.0).astype(jnp.bfloat16)
        xs[...] = jnp.dot(tall, across, preferred_element_type=jnp.float32)

        def group(q, c2):
            base = q * 16
            for r in range(16):
                row = xs[pl.ds(base + r, 1), :]
                value = jnp.where(keep, jnp.broadcast_to(row, (BLK, area)), 0.0)
                wide[t, pl.ds(pl.multiple_of((base + r) * BLK, BLK), BLK), :] = value.astype(jnp.bfloat16)
            return c2

        lax.fori_loop(0, area // 16, group, 0)
        return c

    lax.fori_loop(0, ntiles, widen, 0)

    own_virt.wait()

    def virt_wait(o, c):
        src = (me + o) % 16
        pltpu.make_async_remote_copy(
            src_ref=virt_ref.at[0], dst_ref=virt.at[src],
            send_sem=virt_send.at[o], recv_sem=virt_recv.at[src],
            device_id=(src, red), device_id_type=MESH,
        ).wait()
        return c

    lax.fori_loop(1, 16, virt_wait, 0)

    def spread(t, c):
        pair = virt[t].astype(jnp.float32)
        chosen = jnp.where(listed_ref[0, pl.ds(t, 1), :] == 2 * t, pair[0:1, :], pair[1:2, :])
        split = jnp.where(lane // BLK == sub, jnp.broadcast_to(chosen, (BLK, area)), 0.0)
        block = jnp.dot(split.astype(jnp.bfloat16), along, preferred_element_type=jnp.float32)
        tall = jnp.concatenate([block] * BLK, axis=0)
        kv[t] = jnp.where(same_group, tall, 0.0).astype(jnp.bfloat16)
        return c

    lax.fori_loop(0, ntiles, spread, 0)

    def make_kernel(first, count, begin, end):
        def tile(t, c):
            half = jnp.dot(
                rows[first * naux:(first + count) * naux, :], wide[t], preferred_element_type=jnp.float32
            ).astype(jnp.bfloat16)
            value = jnp.dot(half, kv[t], preferred_element_type=jnp.float32).astype(jnp.bfloat16)
            k0 = {0: 0, 2: 1, 3: 2}[first]
            kern[k0 * naux:(k0 + count) * naux, pl.ds(pl.multiple_of(t * area, area), area)] = value
            return c

        lax.fori_loop(begin, end, tile, 0)

    def product(n):
        row_slot, col_slot = PAIRS[n]
        k0 = {0: 0, 2: 1, 3: 2}[col_slot]
        value = lax.dot_general(
            rows[row_slot * naux:(row_slot + 1) * naux, :], kern[k0 * naux:(k0 + 1) * naux, :],
            (((1,), (1,)), ((), ())), preferred_element_type=jnp.float32,
        )
        tail = value[:, 128:]
        sendbuf[n, 0:naux, :] = value[:, 0:128].astype(jnp.bfloat16)
        folded = jnp.concatenate([tail[i * 16:(i + 1) * 16] for i in range(8)], axis=1)
        sendbuf[n, naux:naux + 16, :] = folded.astype(jnp.bfloat16)
        folded = jnp.concatenate([tail[128:144]] * 8, axis=1)
        sendbuf[n, naux + 16:naux + 32, :] = folded.astype(jnp.bfloat16)

    def part(n):
        return pltpu.make_async_remote_copy(
            src_ref=sendbuf.at[n], dst_ref=recvbuf.at[red],
            send_sem=part_send.at[n], recv_sem=part_recv.at[red],
            device_id=(me, n), device_id_type=MESH,
        )

    def flush(begin, count):
        def one(o, c):
            n = begin + (red + o) % count

            @pl.when(n == red)
            def _():
                pltpu.make_async_copy(sendbuf.at[n], recvbuf.at[red], part_recv.at[red]).start()

            @pl.when(n != red)
            def _():
                part(n).start()

            return c

        lax.fori_loop(0, count, one, 0)

    own_copy.wait()

    def relay(c):
        far[c].wait_recv()
        fwd[c].start()

    relay(0)
    make_kernel(0, 1, 0, 8)
    relay(1)
    for c in range(CHUNKS):
        near[c].start()
    make_kernel(0, 1, 8, 16)
    relay(2)
    sib[2].start()
    sib[0].wait_recv()
    product(0)
    product(1)
    make_kernel(2, 1, 0, 16)
    sib[2].wait_recv()
    for n in range(2, 6):
        product(n)
    flush(0, 6)
    for c in range(CHUNKS):
        fwd[c].wait_recv()
    sib[3].start()
    make_kernel(3, 1, 0, 16)
    product(6)
    product(8)
    sib[3].wait_recv()
    for n in (7, 9, 10):
        product(n)
    flush(6, 5)
    for c in range(CHUNKS):
        near[c].wait_recv()
        near_sib[c].start()
    for n in (11, 13, 15):
        product(n)
    for c in range(CHUNKS):
        near_sib[c].wait_recv()
    for n in (12, 14):
        product(n)
    flush(11, 5)

    total = jnp.zeros(summed.shape, jnp.float32)
    for g in range(16):
        pltpu.make_async_copy(sendbuf.at[0], recvbuf.at[g], part_recv.at[g]).wait()
        total = total + recvbuf[g].astype(jnp.float32)
    summed[...] = total
    final = pltpu.make_async_remote_copy(
        src_ref=summed, dst_ref=arrived, send_sem=final_sem.at[0], recv_sem=final_sem.at[1],
        device_id=(to_pair, to_red), device_id_type=MESH,
    )

    @pl.when(stays)
    def _():
        pltpu.make_async_copy(summed, arrived, final_sem.at[1]).start()

    @pl.when(jnp.logical_not(stays))
    def _():
        final.start()

    pltpu.make_async_copy(summed, arrived, final_sem.at[1]).wait()
    out_ref[:, 0:128] = arrived[0:naux, :]
    for i in range(8):
        out_ref[i * 16:(i + 1) * 16, 128:144] = arrived[naux:naux + 16, i * 16:(i + 1) * 16]
    out_ref[128:144, 128:144] = arrived[naux + 16:naux + 32, 0:16]

    @pl.when(jnp.logical_not(stays))
    def _():
        final.wait_send()

    for c in range(CHUNKS):
        far[c].wait_send()
        fwd[c].wait_send()
        near[c].wait_send()
        near_sib[c].wait_send()
    for i in (0, 2, 3):
        sib[i].wait_send()

    def sent(o, c):
        part((red + o) % 16).wait_send()
        return c

    lax.fori_loop(1, 16, sent, 0)


def shards(three_center, occ_src, occ_block, occ_blocks, virt_block, virt_blocks):
    naux, ntiles, area = three_center.shape
    tiles = three_center.reshape(naux, ntiles * area)
    dma = pltpu.SemaphoreType.DMA
    bf16 = jnp.bfloat16
    return pl.pallas_call(
        kernel,
        out_shape=jax.ShapeDtypeStruct((naux, naux), jnp.float32),
        in_specs=[
            pl.BlockSpec(memory_space=pl.ANY),
        ] + [pl.BlockSpec(memory_space=pltpu.VMEM)] * 5,
        out_specs=pl.BlockSpec(memory_space=pltpu.VMEM),
        scratch_shapes=[
            pltpu.VMEM((8 * naux, ntiles * area), bf16),
            pltpu.VMEM((ntiles, ntiles * area, area), bf16),
            pltpu.VMEM((area, area), jnp.float32),
            pltpu.VMEM((area, area), bf16),
            pltpu.VMEM((ntiles, area, area), bf16),
            pltpu.VMEM((ntiles,) + virt_blocks.shape[1:], bf16),
            pltpu.VMEM((3 * naux, ntiles * area), bf16),
            pltpu.VMEM((16, naux + 32, 128), bf16),
            pltpu.VMEM((16, naux + 32, 128), bf16),
            pltpu.VMEM((naux + 32, 128), jnp.float32),
            pltpu.VMEM((naux + 32, 128), jnp.float32),
            dma((CHUNKS,)), dma((CHUNKS,)), dma((CHUNKS,)), dma((CHUNKS,)),
            dma((CHUNKS,)), dma((CHUNKS,)), dma((CHUNKS,)), dma((CHUNKS,)),
            dma((4,)), dma((4,)), dma((16,)), dma((16,)), dma((16,)), dma((16,)), dma((2,)), dma((2,)),
        ],
        compiler_params=pltpu.CompilerParams(
            collective_id=0, has_side_effects=True, vmem_limit_bytes=64000000
        ),
    )(tiles, occ_src, occ_block, occ_blocks, virt_block, virt_blocks)


def solution(mesh):
    placed = (
        P("pair", "red", None),
        P("red", None),
        P("red", None),
        P("red", None),
        P("red", None, None),
        P("red", "pair", None),
    )
    return jax.shard_map(
        shards, mesh=mesh, in_specs=placed, out_specs=P("pair", "red"), check_vma=False
    )
```

time: 123 us -> 109 us (0.89)
  the two profiles are of different devices: /device:TPU:7 before, /device:TPU:4 now
where the time goes in v2:
time: 109 us; the launch traced here: 108 us
  Pallas kernels  103 us (94%)
  local copies, waits for them, and re-layouts  5.67 us (5%)
    pallas_call x1, Pallas kernels, shards(): pl.pallas_call(kernel, out_shape=jax.ShapeDtypeStruct((naux, naux), jnp.f...  103 us
    unnamed x3, local copies, waits for them, and re-layouts  5.67 us

profile of v2, /device:TPU:4, one launch (start us, length us, event | category | flops | bytes accessed | tf_op | source)
XLA Modules:
  0.0 108.5 jit_solution(14503917808690072755)
XLA Ops:
  0.0 1.3 %copy.7.listed_ref = s32[1,16,1]{2,1,0:T(8,128)} copy(s32[1,16,1]{1,2,0:T(1,128)} %param.10) | data formatting | bytes 128 | tf_op args[4]
  1.3 2.8 %copy.8 = bf16[18,8,16,256]{3,1,2,0:T(8,128)(2,1)} copy(bf16[18,8,16,256]{3,2,1,0:T(8,128)(2,1)} %bitcast.3) | data formatting | bytes 2359296
  4.1 102.8 %shard_map.64 = f32[144,144]{1,0:T(8,128)} custom-call(bf16[144,4096]{1,0:T(8,128)(2,1)} %bitcast.2, s32[16,16]{1,0:T(8,128)} %src_ref.1, s32[16,16]{1,0:T(8,128)} %block_ref.1, bf16[32,256]{1,0:T(8,128)(2,1)} %occ_ref.1, s32[1,16,1]{2,1,0:T(8,128)} %copy.7.listed_ref, bf16[1,2,256]{2,1,0:T(2,128)(2,1)} %virt_ref.1), custom_call_target="tpu_custom_call" | custom-call | tf_op jit(solution)/shard_map/pallas_call | solution.py:354
  106.9 1.6 %copy.10 = f32[144,144]{1,0:T(8,128)} copy(f32[144,144]{1,0:T(8,128)} %shard_map.64) | data formatting | bytes 165888

commit v3 on v2

--- a/solution.py
+++ b/solution.py
@@ -137,6 +137,10 @@
         for c in range(CHUNKS)
     ]
 
+    def relay(c):
+        far[c].wait_recv()
+        fwd[c].start()
+
     lane = lax.broadcasted_iota(jnp.int32, (BLK, area), 1)
     sub = lax.broadcasted_iota(jnp.int32, (BLK, area), 0)
     keep = (lane % BLK) == sub
@@ -185,7 +189,9 @@
         lax.fori_loop(0, area // 16, group, 0)
         return c
 
-    lax.fori_loop(0, ntiles, widen, 0)
+    lax.fori_loop(0, 11, widen, 0)
+    relay(0)
+    lax.fori_loop(11, ntiles, widen, 0)
 
     own_virt.wait()
 
@@ -262,17 +268,12 @@
 
     own_copy.wait()
 
-    def relay(c):
-        far[c].wait_recv()
-        fwd[c].start()
-
-    relay(0)
     make_kernel(0, 1, 0, 8)
     relay(1)
-    for c in range(CHUNKS):
-        near[c].start()
     make_kernel(0, 1, 8, 16)
     relay(2)
+    for c in range(CHUNKS):
+        near[c].start()
     sib[2].start()
     sib[0].wait_recv()
     product(0)

time: 109 us -> 107 us (0.982)
    pallas_call x1, Pallas kernels: 103 us -> 102 us  [shards(): pl.pallas_call(kernel, out_shape=jax.ShapeDtypeStruct((naux, naux), jnp.f...]
where the time goes in v3:
time: 107 us
  Pallas kernels  102 us (95%)
  local copies, waits for them, and re-layouts  5.67 us (5%)
    pallas_call x1, Pallas kernels, shards(): pl.pallas_call(kernel, out_shape=jax.ShapeDtypeStruct((naux, naux), jnp.f...  102 us
    unnamed x3, local copies, waits for them, and re-layouts  5.67 us

profile of v3, /device:TPU:4, one launch (start us, length us, event | category | flops | bytes accessed | tf_op | source)
XLA Modules:
  0.0 107.3 jit_solution(13981563852117749571)
XLA Ops:
  0.0 1.3 %copy.7.listed_ref = s32[1,16,1]{2,1,0:T(8,128)} copy(s32[1,16,1]{1,2,0:T(1,128)} %param.10) | data formatting | bytes 128 | tf_op args[4]
  1.3 2.8 %copy.8 = bf16[18,8,16,256]{3,1,2,0:T(8,128)(2,1)} copy(bf16[18,8,16,256]{3,2,1,0:T(8,128)(2,1)} %bitcast.3) | data formatting | bytes 2359296
  4.1 101.6 %shard_map.64 = f32[144,144]{1,0:T(8,128)} custom-call(bf16[144,4096]{1,0:T(8,128)(2,1)} %bitcast.2, s32[16,16]{1,0:T(8,128)} %src_ref.1, s32[16,16]{1,0:T(8,128)} %block_ref.1, bf16[32,256]{1,0:T(8,128)(2,1)} %occ_ref.1, s32[1,16,1]{2,1,0:T(8,128)} %copy.7.listed_ref, bf16[1,2,256]{2,1,0:T(2,128)(2,1)} %virt_ref.1), custom_call_target="tpu_custom_call" | custom-call | tf_op jit(solution)/shard_map/pallas_call | solution.py:355
  105.7 1.6 %copy.10 = f32[144,144]{1,0:T(8,128)} copy(f32[144,144]{1,0:T(8,128)} %shard_map.64) | data formatting | bytes 165888
